TPU v7x, 32 devices: a whole 2x2x4 slice. The times are simulated.
32 devices in a mesh: batch: 8 (over z, y), head: 4 (over x, core).
Axes of the slice: x: 2, y: 2, z: 4, core: 2. Of those that a mesh axis runs over, the one named last changes fastest.
Arguments:
- tokens: bfloat16 [16384, 768], P(('batch', 'head')), may hold values from -6 to 6
- cotangent: bfloat16 [16384, 768], P(('batch', 'head')), may hold values from -6 to 6
- lengths: int32 [32], P('batch'), may hold values from 16 to 512, as said below
- labels: int32 [32], P('batch'), may hold values from 0 to 2
- w_qkv: bfloat16 [768, 2304], replicated, may hold values from -0.21875 to 0.21875
- w_out: bfloat16 [768, 768], replicated, may hold values from -0.875 to 0.875
- w_up: bfloat16 [768, 3072], replicated, may hold values from -0.21875 to 0.21875
- w_down: bfloat16 [3072, 768], replicated, may hold values from -0.109375 to 0.109375
- w_pool: bfloat16 [768, 768], replicated, may hold values from -0.21875 to 0.21875
- w_class: bfloat16 [3, 768], replicated, may hold values from -0.625 to 0.625
- biases: float32 [7, 768], replicated, may hold values from -3 to 3
- norm_gains: float32 [2, 768], replicated, may hold values from 0.25 to 1.75
- bias_up: float32 [3072], replicated, may hold values from -3 to 3
Outputs:
- out: bfloat16 [16384, 768], P(('batch', 'head'))
- grad_tokens: bfloat16 [16384, 768], P(('batch', 'head'))
- losses: float32 [32], P(('batch', 'head'))
- g_qkv: float32 [768, 2304], P(None, ('batch', 'head'))
- g_out: float32 [768, 768], P(None, ('batch', 'head'))
- g_up: float32 [768, 3072], P(None, ('batch', 'head'))
- g_down: float32 [3072, 768], P(None, ('batch', 'head'))
- g_pool: float32 [768, 768], P(None, ('batch', 'head'))
- g_class: float32 [3, 768], P(None, ('batch', 'head'))
- g_biases: float32 [6, 768], P(None, ('batch', 'head'))
- g_gains: float32 [2, 768], P(None, ('batch', 'head'))
- g_bias_up: float32 [3072], P(('batch', 'head'))
- g_pool_bias: float32 [768], P(('batch', 'head'))
Inputs may be any that keep to these rules, and one draw needn't show every extreme that they name: `lengths`: some sequence has exactly 512 and some exactly 16 positions.
All inputs are finite; a program needn't handle non-finite values.
Results may differ from a plain program's by a relative error of at most 0.014.
Values may be sent and summed in bfloat16 or wider, within the bound.
A program may use at most 192 MiB of HBM per device.

v0:
```python
import jax
import jax.numpy as jnp
from jax import lax
from jax.sharding import PartitionSpec as P

D = 768
HEADS = 12
HEAD_DIM = 64
CLASSES = 3
SLOT = 512


def layer_norm(hidden, gain, shift):
    center = hidden - jnp.mean(hidden, axis=-1, keepdims=True)
    spread = jnp.mean(center * center, axis=-1, keepdims=True)
    return center * lax.rsqrt(spread + 1e-12) * gain + shift


def exact_gelu(hidden):
    return jax.nn.gelu(hidden, approximate=False)


def inner(left, right):
    return lax.dot_general(
        left, right, (((0,), (0,)), ((), ())), preferred_element_type=jnp.float32
    )


def against(left, right):
    return lax.dot_general(
        left, right, (((1,), (1,)), ((), ())), preferred_element_type=jnp.float32
    )


def exact(left, right):
    return jnp.dot(left, right, precision=lax.Precision.HIGHEST, preferred_element_type=jnp.float32)


def masked_scores(queries, keys_all, length):
    scores = jnp.einsum(
        "qhd,khd->hqk", queries, keys_all, preferred_element_type=jnp.float32
    ) * HEAD_DIM ** (-0.5)
    allowed = jnp.arange(SLOT) < length
    return jnp.where(allowed[None, None, :], scores, -1e30)


def attend_forward(seq_item):
    packed, length = seq_item
    queries = packed[:, 0]
    keys_all = packed[:, 1]
    values = packed[:, 2]
    scores = masked_scores(queries, keys_all, length)
    row_max = jnp.max(scores, axis=-1, keepdims=True)
    exp_sum = jnp.sum(jnp.exp(scores - row_max), axis=-1, keepdims=True)
    log_total = row_max + jnp.log(exp_sum)
    weights = jnp.exp(scores - log_total).astype(jnp.bfloat16)
    context = jnp.einsum("hqk,khd->qhd", weights, values, preferred_element_type=jnp.float32)
    return (context.astype(jnp.bfloat16), log_total)


def attend_backward(seq_item):
    packed, log_total, d_context, length = seq_item
    queries = packed[:, 0]
    keys_all = packed[:, 1]
    values = packed[:, 2]
    scores = masked_scores(queries, keys_all, length)
    weights = jnp.exp(scores - log_total)
    weights_low = weights.astype(jnp.bfloat16)
    d_weights = jnp.einsum("qhd,khd->hqk", d_context, values, preferred_element_type=jnp.float32)
    d_values = jnp.einsum(
        "hqk,qhd->khd", weights_low, d_context, preferred_element_type=jnp.float32
    )
    row_dot = jnp.sum(weights * d_weights, axis=-1, keepdims=True)
    d_scores = (weights * (d_weights - row_dot)).astype(jnp.bfloat16)
    d_queries = jnp.einsum(
        "hqk,khd->qhd", d_scores, keys_all, preferred_element_type=jnp.float32
    ) * HEAD_DIM ** (-0.5)
    d_keys = jnp.einsum(
        "hqk,qhd->khd", d_scores, queries, preferred_element_type=jnp.float32
    ) * HEAD_DIM ** (-0.5)
    return jnp.stack([d_queries, d_keys, d_values], axis=1).astype(jnp.bfloat16)


def per_device(
    tokens,
    cotangent,
    lengths,
    labels,
    w_qkv,
    w_out,
    w_up,
    w_down,
    w_pool,
    w_class,
    biases,
    norm_gains,
    bias_up,
):
    head_parts = lax.axis_size("head")
    head_rank = lax.axis_index("head")
    tok_rows = tokens.shape[0]
    own_seqs = tok_rows // SLOT
    local_heads = HEADS // head_parts
    slice_width = D // head_parts
    own_lengths = lax.dynamic_slice_in_dim(lengths, head_rank * own_seqs, own_seqs)
    own_labels = lax.dynamic_slice_in_dim(labels, head_rank * own_seqs, own_seqs)
    slot_live = (
        (jnp.arange(SLOT)[None, :] < own_lengths[:, None]).reshape(tok_rows).astype(jnp.float32)
    )
    zeros_key = jnp.zeros((D,), jnp.float32)
    packed = jnp.dot(tokens, w_qkv, preferred_element_type=jnp.float32) + jnp.concatenate(
        [biases[0], zeros_key, biases[1]]
    )
    packed_low = packed.astype(jnp.bfloat16)
    head_view = lax.all_to_all(
        packed_low.reshape(tok_rows, 3, head_parts, slice_width),
        "head",
        split_axis=2,
        concat_axis=0,
        tiled=True,
    )
    seq_view = head_view.reshape(head_parts * own_seqs, SLOT, 3, local_heads, HEAD_DIM)
    context, log_total = lax.map(attend_forward, (seq_view, lengths))
    context_back = lax.all_to_all(
        context.reshape(head_parts * tok_rows, 1, slice_width),
        "head",
        split_axis=0,
        concat_axis=1,
        tiled=True,
    )
    context_tok = context_back.reshape(tok_rows, D)
    attn = jnp.dot(context_tok, w_out, preferred_element_type=jnp.float32) + biases[2]
    first_sum = tokens.astype(jnp.float32) + attn
    norm_one, first_pull = jax.vjp(layer_norm, first_sum, norm_gains[0], biases[3])
    norm_low = norm_one.astype(jnp.bfloat16)
    hidden_up = jnp.dot(norm_low, w_up, preferred_element_type=jnp.float32) + bias_up
    activated_full, gelu_pull = jax.vjp(exact_gelu, hidden_up)
    activated = activated_full.astype(jnp.bfloat16)
    branch = jnp.dot(activated, w_down, preferred_element_type=jnp.float32) + biases[4]
    out_full, second_pull = jax.vjp(layer_norm, norm_one + branch, norm_gains[1], biases[5])
    leading = out_full.reshape(own_seqs, SLOT, D)[:, 0].astype(jnp.bfloat16)
    pooled = jnp.tanh(jnp.dot(leading, w_pool, preferred_element_type=jnp.float32) + biases[6])
    pooled_low = pooled.astype(jnp.bfloat16)
    logits = against(pooled_low, w_class)
    onehot = (jnp.arange(CLASSES)[None, :] == own_labels[:, None]).astype(jnp.float32)
    losses = jax.nn.logsumexp(logits, axis=-1) - jnp.sum(onehot * logits, axis=-1)
    d_logits = jax.nn.softmax(logits, axis=-1) - onehot
    g_class = exact(d_logits.T, pooled_low.astype(jnp.float32))
    d_pre = exact(d_logits, w_class.astype(jnp.float32)) * (1.0 - pooled * pooled)
    g_pool = exact(leading.astype(jnp.float32).T, d_pre)
    g_pool_bias = jnp.sum(d_pre, axis=0)
    d_leading = exact(d_pre, w_pool.astype(jnp.float32).T)
    d_out = cotangent.astype(jnp.float32) * slot_live[:, None]
    d_out = d_out.reshape(own_seqs, SLOT, D).at[:, 0].add(d_leading).reshape(tok_rows, D)
    d_h2, g_gain_two, g_shift_two = second_pull(d_out)
    d_branch = d_h2.astype(jnp.bfloat16)
    g_bias_down = jnp.sum(d_branch.astype(jnp.float32), axis=0)
    g_down = inner(activated, d_branch)
    d_activated = against(d_branch, w_down)
    d_up = gelu_pull(d_activated)[0].astype(jnp.bfloat16)
    g_bias_up = jnp.sum(d_up.astype(jnp.float32), axis=0)
    g_up = inner(norm_low, d_up)
    d_norm_one = d_h2 + against(d_up, w_up)
    d_h1, g_gain_one, g_shift_one = first_pull(d_norm_one)
    d_attn = d_h1.astype(jnp.bfloat16)
    g_bias_out = jnp.sum(d_attn.astype(jnp.float32), axis=0)
    g_out = inner(context_tok, d_attn)
    d_context = against(d_attn, w_out).astype(jnp.bfloat16)
    d_context_heads = lax.all_to_all(
        d_context.reshape(tok_rows, head_parts, slice_width),
        "head",
        split_axis=1,
        concat_axis=0,
        tiled=True,
    )
    d_context_seq = d_context_heads.reshape(head_parts * own_seqs, SLOT, local_heads, HEAD_DIM)
    d_seq = lax.map(attend_backward, (seq_view, log_total, d_context_seq, lengths))
    d_back = lax.all_to_all(
        d_seq.reshape(head_parts * tok_rows, 3, 1, slice_width),
        "head",
        split_axis=0,
        concat_axis=2,
        tiled=True,
    )
    d_packed = d_back.reshape(tok_rows, 3 * D)
    g_qkv = inner(tokens, d_packed)
    column_sums = jnp.sum(d_packed.astype(jnp.float32), axis=0)
    grad_tokens = (d_h1 + against(d_packed, w_qkv)).astype(jnp.bfloat16)
    g_biases = jnp.stack(
        [column_sums[:D], column_sums[2 * D :], g_bias_out, g_shift_one, g_bias_down, g_shift_two]
    )
    g_gains = jnp.stack([g_gain_one, g_gain_two])
    g_qkv, g_out, g_up, g_down, g_pool, g_class, g_biases, g_gains, g_bias_up, g_pool_bias = (
        lax.psum_scatter(g_qkv, ("batch", "head"), scatter_dimension=1, tiled=True),
        lax.psum_scatter(g_out, ("batch", "head"), scatter_dimension=1, tiled=True),
        lax.psum_scatter(g_up, ("batch", "head"), scatter_dimension=1, tiled=True),
        lax.psum_scatter(g_down, ("batch", "head"), scatter_dimension=1, tiled=True),
        lax.psum_scatter(g_pool, ("batch", "head"), scatter_dimension=1, tiled=True),
        lax.psum_scatter(g_class, ("batch", "head"), scatter_dimension=1, tiled=True),
        lax.psum_scatter(g_biases, ("batch", "head"), scatter_dimension=1, tiled=True),
        lax.psum_scatter(g_gains, ("batch", "head"), scatter_dimension=1, tiled=True),
        lax.psum_scatter(g_bias_up, ("batch", "head"), scatter_dimension=0, tiled=True),
        lax.psum_scatter(g_pool_bias, ("batch", "head"), scatter_dimension=0, tiled=True),
    )
    return (
        out_full.astype(jnp.bfloat16),
        grad_tokens,
        losses,
        g_qkv,
        g_out,
        g_up,
        g_down,
        g_pool,
        g_class,
        g_biases,
        g_gains,
        g_bias_up,
        g_pool_bias,
    )


def solution(mesh):
    return jax.shard_map(
        per_device,
        mesh=mesh,
        in_specs=(
            P(("batch", "head"), None),
            P(("batch", "head"), None),
            P("batch"),
            P("batch"),
            P(),
            P(),
            P(),
            P(),
            P(),
            P(),
            P(),
            P(),
            P(),
        ),
        out_specs=(
            P(("batch", "head"), None),
            P(("batch", "head"), None),
            P(("batch", "head")),
            P(None, ("batch", "head")),
            P(None, ("batch", "head")),
            P(None, ("batch", "head")),
            P(None, ("batch", "head")),
            P(None, ("batch", "head")),
            P(None, ("batch", "head")),
            P(None, ("batch", "head")),
            P(None, ("batch", "head")),
            P(("batch", "head")),
            P(("batch", "head")),
        ),
        check_vma=False,
    )
```

profile of v0, /device:TPU:0, one launch (start us, length us, event | category | flops | bytes accessed | tf_op | source)
XLA Modules:
  0.0 791.8 jit_solution(17786111128805935081)
XLA Ops:
  9.3 4.5 fusion.34
  21.3 4.7 all-to-all-start
  26.0 29.1 %all-to-all-done = bf16[512,3,4,192]{0,3,1,2:T(8,128)(2,1)} async-done(((bf16[512,3,4,192]{0,3,1,2:T(8,128)(2,1)}), bf16[512,3,4,192]{0,3,1,2:T(8,128)(2,1)}, u32[]{:S(2)}, u32[]{:S(2)}) %all-to-all-start) | async-done | bytes 2359328 | tf_op jit(solution)/shard_map/all_to_all | solution.py:115
  55.1 24.0 %while.23 = (s32[]{:T(128)}, bf16[4,512,3,64]{1,3,2,0:T(8,128)(2,1)}, f32[4,3,512,1]{2,1,3,0:T(4,128)}, bf16[4,512,3,3,64]{1,4,3,2,0:T(8,128)(2,1)}, s32[4]{0:T(128)S(1)}, /*index=5*/s32[]{:T(128)}) while((s32[]{:T(128)}, bf16[4,512,3,64]{1,3,2,0:T(8,128)(2,1)}, f32[4,3,512,1]{2,1,3,0:T(4,128)}, bf16[4,512,3,3,64]{1,4,3,2,0:T(8,128)(2,1)}, ...), condition=%wide.region_3.4_spmd, body=%wide.region_0.3_spmd.sunk | while | flops 210074624 | bytes 11459673 | solution.py:123
  104.6 5.5 all-to-all-done.1
  114.3 5.7 copy.67
  128.2 19.6 %multiply_convert_fusion.1 = (bf16[512,3072]{1,0:T(8,128)(2,1)S(1)}, f32[512,3072]{1,0:T(8,128)}, f32[512,3072]{1,0:T(8,128)}) fusion(f32[3072]{0:T(1024)S(1)} %copy-done.37, bf16[768,3072]{1,0:T(8,128)(2,1)} %param.25, f32[512,768]{1,0:T(8,128)S(1)} %get-tuple-element.165, f32[768]{0:T(1024)S(1)} %copy-done.32, f32[768]{0:T(1024)S(1)} %get-tuple-element.176, ...), kind=kOutput, calls=%fused_computation.50 | convolution fusion | flops 2521694208 | bytes 22042624 | tf_op jit(solution)/shard_map/dot_general | solution.py:136
  172.7 9.5 %convert_reduce_fusion = (f32[3072]{0:T(1024)}, bf16[512,3072]{1,0:T(8,128)(2,1)S(1)}) fusion(f32[512,3072]{1,0:T(8,128)} %get-tuple-element.156, f32[512,3072]{1,0:T(8,128)} %get-tuple-element.166, f32[3072]{0:T(1024)} %param.31, bf16[512,768]{1,0:T(8,128)(2,1)S(1)} %get-tuple-element.148, bf16[3072,768]{1,0:T(8,128)(2,1)} %param.26), kind=kOutput, calls=%fused_computation.48 | convolution fusion | flops 2442654720 | bytes 21258240 | tf_op jit(solution)/shard_map/dot_general | solution.py:30
  182.2 7.3 multiply_reduce_fusion.2
  204.6 7.8 all-to-all-done.2
  212.4 39.9 %while.24 = (s32[]{:T(128)}, bf16[4,512,3,3,64]{1,4,3,2,0:T(8,128)(2,1)}, bf16[4,512,3,3,64]{1,4,3,2,0:T(8,128)(2,1)}, s32[4]{0:T(128)}, f32[4,3,512,1]{2,1,3,0:...) while((s32[]{:T(128)}, bf16[4,512,3,3,64]{1,4,3,2,0:T(8,128)(2,1)}, ...), condition=%wide.region_16.17_spmd, body=%wide.region_14.16_spmd.sunk | while | flops 512654336 | bytes 27953856 | solution.py:177
  252.3 4.9 copy.70
  257.2 5.9 reshape.346
  263.1 7.0 copy.71
  270.0 53.9 %all_to_all.60 = bf16[2048,3,1,192]{3,1,2,0:T(4,128)(2,1)} all-to-all(bf16[2048,3,1,192]{3,1,2,0:T(4,128)(2,1)} %copy.71), channel_id=1, replica_groups=mesh['batch'=8,'head'=4] {'head'}, dimensions={0} | all-to-all | bytes 4718592 | tf_op jit(solution)/shard_map/all_to_all | solution.py:178
  323.9 7.4 copy.80
  335.0 5.0 convolution_bitcast_fusion
  340.2 8.8 %fusion.48 = f32[768,3072]{0,1:T(8,128)} fusion(bf16[512,3072]{1,0:T(8,128)(2,1)} %copy-done.43, f32[512,768]{1,0:T(8,128)} %copy-done.6, f32[768]{0:T(1024)} %get-tuple-element.107, f32[768]{0:T(1024)S(1)} %copy-done.27, f32[512]{0:T(512)} %copy-done.28, f32[512]{0:T(512)S(1)} %copy-done.17), kind=kOutput, calls=%fused_computation.138 | convolution fusion | flops 2417885184 | bytes 14166016 | tf_op jit(solution)/shard_map/dot_general | solution.py:24
  349.1 8.4 %fusion.61 = f32[3072,768]{0,1:T(8,128)} fusion(bf16[512,3072]{1,0:T(8,128)(2,1)} %copy-done.42, bf16[512,768]{1,0:T(8,128)(2,1)} %copy-done.13), kind=kOutput, calls=%fused_computation.148 | convolution fusion | flops 2415919104 | bytes 13369344 | tf_op jit(solution)/shard_map/dot_general | solution.py:24
  375.8 42.2 %all-reduce.5 = (f32[3,768]{1,0:T(4,128)}, f32[6,768]{1,0:T(8,128)}, f32[2,768]{1,0:T(2,128)}, f32[3072]{0:T(1024)}, f32[768]{0:T(1024)}) all-reduce(f32[3,768]{1,0:T(4,128)S(1)} %broadcast_multiply_fusion.1, f32[6,768]{1,0:T(8,128)} %stack.38, ...), channel_id=7, replica_groups=mesh['batch'=8,'head'=4] {'batch','head'}, use_global_device_ids=true, to_apply=%region_24.25.clone | all-reduce | flops 12288 | bytes 98304
  424.6 5.1 add_convert_fusion.1
  429.7 70.9 %reduce-scatter.9.cloned.1.call-done = f32[768,72]{0,1:T(8,128)} async-done(((f32[768,2304]{0,1:T(8,128)}), f32[768,72]{0,1:T(8,128)}) %reduce-scatter.9.cloned.1.call-update) | async-done | bytes 221200 | tf_op jit(solution)/shard_map/reduce_scatter | solution.py:194
  500.6 142.2 %reduce-scatter.13.cloned.1.call-done = f32[768,96]{0,1:T(8,128)} async-done(((f32[768,3072]{0,1:T(8,128)}), f32[768,96]{0,1:T(8,128)}) %reduce-scatter.13.cloned.1.call-update) | async-done | bytes 294928 | tf_op jit(solution)/shard_map/reduce_scatter | solution.py:196
  642.8 140.9 %reduce-scatter.15.cloned.1.call-done = f32[3072,24]{0,1:T(8,128)} async-done(((f32[3072,768]{0,1:T(8,128)}), f32[3072,24]{0,1:T(8,128)}) %reduce-scatter.15.cloned.1.call-update) | async-done | bytes 294928 | tf_op jit(solution)/shard_map/reduce_scatter | solution.py:197
  (262 shorter events, 176.7 us)
Async XLA Ops:
  8.8 139.0 %copy-start.26 = (f32[768]{0:T(1024)}, f32[768]{0:T(1024)S(1)}, u32[]{:S(2)}) copy-start(f32[768]{0:T(1024)S(1)} %get-tuple-element.176) | copy-start | bytes 9220
  21.3 33.8 %copy-start.40 = (s32[4]{0:T(128)S(1)}, s32[4]{0:T(128)}, u32[]{:S(2)}) copy-start(s32[4]{0:T(128)} %param.21) | copy-start | bytes 52
  21.3 33.8 %all-to-all-start = ((bf16[512,3,4,192]{0,3,1,2:T(8,128)(2,1)}), bf16[512,3,4,192]{0,3,1,2:T(8,128)(2,1)}, u32[]{:S(2)}, u32[]{:S(2)}) async-start(bf16[512,3,4,192]{0,3,1,2:T(8,128)(2,1)} %copy.64), calls=%async_computation | async-start | bytes 4718592 | tf_op jit(solution)/shard_map/all_to_all | solution.py:115
  85.1 15.2 %copy-start.39 = (s32[4]{0:T(128)S(1)}, s32[4]{0:T(128)}, u32[]{:S(2)}) copy-start(s32[4]{0:T(128)} %param.22) | copy-start | bytes 52
  94.3 15.9 %all-to-all-start.1 = ((bf16[4,2,49152]{2,1,0:T(2,128)(2,1)}), bf16[4,2,49152]{2,1,0:T(2,128)(2,1)}, u32[]{:S(2)}, u32[]{:S(2)}) async-start(bf16[4,2,49152]{2,1,0:T(2,128)(2,1)} %reshape.384), calls=%async_computation.1 | async-start | bytes 1572864 | tf_op jit(solution)/shard_map/all_to_all | solution.py:124
  98.5 331.2 %reduce-scatter.17.cloned.1.call-start = ((), (), s32[]{:S(2)}) async-start(), calls=%async_computation.13 | async-start | bytes 2433024 | tf_op jit(solution)/shard_map/reduce_scatter | solution.py:198
  114.3 10.0 %copy-start.34 = (f32[768]{0:T(1024)S(1)}, f32[768]{0:T(1024)}, u32[]{:S(2)}) copy-start(f32[768]{0:T(1024)} %get-tuple-element.108) | copy-start | bytes 9220
  124.4 23.6 %slice-start = ((s8[4718592]{0:T(1024)(128)(4,1)}), s8[4194304]{0:T(1024)(128)(4,1)S(1)}, s32[]{:S(2)}) async-start(s8[4718592]{0:T(1024)(128)(4,1)} %bitcast.202), calls=%async_computation.14 | async-start | bytes 8388608
  127.1 20.8 %copy-start.6 = (f32[512,768]{1,0:T(8,128)}, f32[512,768]{1,0:T(8,128)S(1)}, u32[]{:S(2)}) copy-start(f32[512,768]{1,0:T(8,128)S(1)} %get-tuple-element.165) | copy-start | bytes 4718596
  127.1 20.8 %copy-start.16 = (f32[512]{0:T(512)}, f32[512]{0:T(512)S(1)}, u32[]{:S(2)}) copy-start(f32[512]{0:T(512)S(1)} %broadcast_multiply_fusion.3) | copy-start | bytes 6148
  128.2 19.7 %copy-start.28 = (f32[512]{0:T(512)}, f32[512]{0:T(512)S(1)}, u32[]{:S(2)}) copy-start(f32[512]{0:T(512)S(1)} %fusion.43) | copy-start | bytes 6148
  128.2 19.7 %copy-start.33 = (f32[768]{0:T(1024)S(1)}, f32[768]{0:T(1024)}, u32[]{:S(2)}) copy-start(f32[768]{0:T(1024)} %get-tuple-element.106) | copy-start | bytes 9220
  128.2 19.7 %slice-start.1 = ((s8[4718592]{0:T(1024)(128)(4,1)}), s8[524288]{0:T(1024)(128)(4,1)S(1)}, s32[]{:S(2)}) async-start(s8[4718592]{0:T(1024)(128)(4,1)} %bitcast.202), calls=%async_computation.15 | async-start | bytes 1048576
  150.7 10.5 %copy-start.1 = (f32[512,768]{1,0:T(8,128)}, f32[512,768]{1,0:T(8,128)S(1)}, u32[]{:S(2)}) copy-start(f32[512,768]{1,0:T(8,128)S(1)} %get-tuple-element.168) | copy-start | bytes 4718596
  150.8 10.5 %copy-start.25 = (f32[768]{0:T(1024)S(1)}, f32[768]{0:T(1024)}, u32[]{:S(2)}) copy-start(f32[768]{0:T(1024)} %slice_reduce_fusion) | copy-start | bytes 9220
  172.6 9.6 %copy-start.13 = (bf16[512,768]{1,0:T(8,128)(2,1)}, bf16[512,768]{1,0:T(8,128)(2,1)S(1)}, u32[]{:S(2)}) copy-start(bf16[512,768]{1,0:T(8,128)(2,1)S(1)} %get-tuple-element.148) | copy-start | bytes 2359300
  172.6 9.6 %copy-start.7 = (f32[512,768]{1,0:T(8,128)S(1)}, f32[512,768]{1,0:T(8,128)}, u32[]{:S(2)}) copy-start(f32[512,768]{1,0:T(8,128)} %copy-done.6) | copy-start | bytes 4718596
  172.6 9.6 %copy-start.9 = (f32[512,768]{1,0:T(8,128)S(1)}, f32[512,768]{1,0:T(8,128)}, u32[]{:S(2)}) copy-start(f32[512,768]{1,0:T(8,128)} %get-tuple-element.154) | copy-start | bytes 4718596
  196.5 15.9 %all-to-all-start.2 = ((bf16[512,4,192]{0,2,1:T(8,128)(2,1)}), bf16[512,4,192]{0,2,1:T(8,128)(2,1)}, u32[]{:S(2)}, u32[]{:S(2)}) async-start(bf16[512,4,192]{0,2,1:T(8,128)(2,1)} %bitcast.198), calls=%async_computation.2 | async-start | bytes 1572864 | tf_op jit(solution)/shard_map/all_to_all | solution.py:169
  200.7 229.0 %reduce-scatter.11.cloned.1.call-start = ((), (), s32[]{:S(2)}) async-start(), calls=%async_computation.10 | async-start | bytes 2433024 | tf_op jit(solution)/shard_map/reduce_scatter | solution.py:195
  204.6 296.0 %reduce-scatter.9.cloned.1.call-start = ((), (), s32[]{:S(2)}) async-start(), calls=%async_computation.9 | async-start | bytes 7299072 | tf_op jit(solution)/shard_map/reduce_scatter | solution.py:194
  339.9 302.9 %reduce-scatter.13.cloned.1.call-start = ((), (), s32[]{:S(2)}) async-start(), calls=%async_computation.11 | async-start | bytes 9732096 | tf_op jit(solution)/shard_map/reduce_scatter | solution.py:196
  349.1 434.6 %reduce-scatter.15.cloned.1.call-start = ((), (), s32[]{:S(2)}) async-start(), calls=%async_computation.12 | async-start | bytes 9732096 | tf_op jit(solution)/shard_map/reduce_scatter | solution.py:197
  358.2 17.6 %copy-start.24 = (f32[768]{0:T(1024)S(1)}, f32[768]{0:T(1024)}, u32[]{:S(2)}) copy-start(f32[768]{0:T(1024)} %get-tuple-element.172) | copy-start | bytes 9220
  (33 other events, 114.5 us)
Sparse Core Ops, SparseCore 0:
  171.1 100.1 reduce-scatter.16
  278.1 98.0 reduce-scatter.10
  382.4 118.0 reduce-scatter.8
  507.9 134.8 reduce-scatter.12
  649.1 134.5 reduce-scatter.14
where the time goes:
time: 800 us; the launch traced here: 792 us
  waiting for transfers between devices  397 us (50%)
  matrix products  112 us (14%)
  local copies, waits for them, and re-layouts  111 us (14%)
  blocking collectives  96.1 us (12%)
  other arithmetic  42.7 us (5%)
  between operations  18.5 us (2%)
  starting transfers between devices  14.2 us (2%)
    reduce_scatter x1, waiting for transfers between devices, per_device(): lax.psum_scatter(g_up, ('batch', 'head'), scatter_dimension=1, tiled=True)  142 us
    reduce_scatter x1, waiting for transfers between devices, per_device(): lax.psum_scatter(g_down, ('batch', 'head'), scatter_dimension=1, tiled=True)  141 us
    reduce_scatter x1, waiting for transfers between devices, per_device(): lax.psum_scatter(g_qkv, ('batch', 'head'), scatter_dimension=1, tiled=True)  70.9 us
    all_to_all x1, blocking collectives, per_device(): lax.all_to_all(d_seq.reshape(head_parts * tok_rows, 3, 1, slice_width), '...  53.9 us
    unnamed x1, blocking collectives  42.2 us
    all_to_all x1, waiting for transfers between devices, per_device(): lax.all_to_all(packed_low.reshape(tok_rows, 3, head_parts, slice_width),...  29.1 us
    dot_general x4, matrix products, inner(): lax.dot_general(left, right, (((0,), (0,)), ((), ())), preferred_element_...  25.8 us
    dot_general x5, matrix products, against(): lax.dot_general(left, right, (((1,), (1,)), ((), ())), preferred_element_...  24.3 us
  transfers between devices with their start and end apart: 8, of which 6 were waited for; matrix products, arithmetic and copies ran while one was open for 19% of the time, Pallas kernels for 0%

commit v1 on v0

--- a/solution.py
+++ b/solution.py
@@ -121,13 +121,21 @@
     )
     seq_view = head_view.reshape(head_parts * own_seqs, SLOT, 3, local_heads, HEAD_DIM)
     context, log_total = lax.map(attend_forward, (seq_view, lengths))
-    context_back = lax.all_to_all(
-        context.reshape(head_parts * tok_rows, 1, slice_width),
-        "head",
-        split_axis=0,
-        concat_axis=1,
-        tiled=True,
-    )
+    x = context.reshape(head_parts * tok_rows, 1, slice_width)
+    ways, here = (lax.axis_size("head"), lax.axis_index("head"))
+    width = x.shape[0] // ways
+    shape = list(x.shape)
+    shape[0] = width
+    height = shape[1]
+    shape[1] = height * ways
+    context_back = jnp.zeros(shape, x.dtype)
+    for mask in range(ways):
+        part = lax.dynamic_slice_in_dim(x, (here ^ mask) * width, width, axis=0)
+        if mask:
+            part = lax.ppermute(part, "head", [(d, d ^ mask) for d in range(ways)])
+        context_back = lax.dynamic_update_slice_in_dim(
+            context_back, part, (here ^ mask) * height, axis=1
+        )
     context_tok = context_back.reshape(tok_rows, D)
     attn = jnp.dot(context_tok, w_out, preferred_element_type=jnp.float32) + biases[2]
     first_sum = tokens.astype(jnp.float32) + attn

time: 800 us -> 779 us (0.974)
  local copies, waits for them, and re-layouts: 111 us -> 98 us
    unnamed x98 -> x85, local copies, waits for them, and re-layouts: 23.3 us -> 11.9 us
    all_to_all x3 -> x0, local copies, waits for them, and re-layouts: 9.99 us -> none  [per_device(): lax.all_to_all(context.reshape(head_parts * tok_rows, 1, slice_width), 'h...]
  transfers between devices with their start and end apart: 8 -> 10, of which waited for: 6 -> 7; matrix products, arithmetic and copies ran while one was open for 19% -> 20% of each run, Pallas kernels for 0% -> 0%
where the time goes in v1:
time: 779 us; the launch traced here: 774 us
  waiting for transfers between devices  396 us (51%)
  matrix products  113 us (15%)
  local copies, waits for them, and re-layouts  98 us (13%)
  blocking collectives  96.3 us (12%)
  other arithmetic  40.8 us (5%)
  between operations  18.3 us (2%)
  starting transfers between devices  11.7 us (2%)
    reduce_scatter x1, waiting for transfers between devices, per_device(): lax.psum_scatter(g_up, ('batch', 'head'), scatter_dimension=1, tiled=True)  142 us
    reduce_scatter x1, waiting for transfers between devices, per_device(): lax.psum_scatter(g_down, ('batch', 'head'), scatter_dimension=1, tiled=True)  141 us
    reduce_scatter x1, waiting for transfers between devices, per_device(): lax.psum_scatter(g_qkv, ('batch', 'head'), scatter_dimension=1, tiled=True)  70.7 us
    all_to_all x1, blocking collectives, per_device(): lax.all_to_all(d_seq.reshape(head_parts * tok_rows, 3, 1, slice_width), '...  53.9 us
    unnamed x1, blocking collectives  42.4 us
    all_to_all x1, waiting for transfers between devices, per_device(): lax.all_to_all(packed_low.reshape(tok_rows, 3, head_parts, slice_width),...  27.5 us
    dot_general x4, matrix products, inner(): lax.dot_general(left, right, (((0,), (0,)), ((), ())), preferred_element_...  25.8 us
    dot_general x5, matrix products, against(): lax.dot_general(left, right, (((1,), (1,)), ((), ())), preferred_element_...  24.3 us
  transfers between devices with their start and end apart: 10, of which 7 were waited for; matrix products, arithmetic and copies ran while one was open for 20% of the time, Pallas kernels for 0%

profile of v1, /device:TPU:0, one launch (start us, length us, event | category | flops | bytes accessed | tf_op | source)
XLA Modules:
  0.0 773.8 jit_solution(1841734559492779505)
XLA Ops:
  9.3 4.5 fusion.34
  13.9 4.3 copy.59
  21.4 4.7 all-to-all-start
  27.7 27.5 %all-to-all-done = bf16[512,3,4,192]{0,3,1,2:T(8,128)(2,1)} async-done(((bf16[512,3,4,192]{0,3,1,2:T(8,128)(2,1)}), bf16[512,3,4,192]{0,3,1,2:T(8,128)(2,1)}, u32[]{:S(2)}, u32[]{:S(2)}) %all-to-all-start) | async-done | bytes 2359328 | tf_op jit(solution)/shard_map/all_to_all | solution.py:115
  55.2 26.6 %while.23 = (s32[]{:T(128)}, bf16[4,512,3,64]{1,3,2,0:T(8,128)(2,1)}, f32[4,3,512,1]{2,1,3,0:T(4,128)}, bf16[4,512,3,3,64]{1,4,3,2,0:T(8,128)(2,1)}, s32[4]{0:T(128)}, /*index=5*/s32[]{:T(128)}) while((s32[]{:T(128)}, bf16[4,512,3,64]{1,3,2,0:T(8,128)(2,1)}, f32[4,3,512,1]{2,1,3,0:T(4,128)}, bf16[4,512,3,3,64]{1,4,3,2,0:T(8,128)(2,1)}, ...), condition=%wide.region_3.4_spmd, body=%wide.region_0.3_spmd.sunk | while | flops 210074624 | bytes 11459673 | solution.py:123
  110.0 20.0 %multiply_convert_fusion.1 = (bf16[512,3072]{1,0:T(8,128)(2,1)S(1)}, f32[512,3072]{1,0:T(8,128)}, f32[512,3072]{1,0:T(8,128)}) fusion(f32[3072]{0:T(1024)S(1)} %copy-done.33, bf16[768,3072]{1,0:T(8,128)(2,1)} %param.25, f32[512,768]{1,0:T(8,128)S(1)} %get-tuple-element.169, f32[768]{0:T(1024)S(1)} %copy-done.29, f32[768]{0:T(1024)S(1)} %get-tuple-element.180, ...), kind=kOutput, calls=%fused_computation.50 | convolution fusion | flops 2521694208 | bytes 22042624 | tf_op jit(solution)/shard_map/dot_general | solution.py:144
  154.8 9.5 %convert_reduce_fusion = (f32[3072]{0:T(1024)}, bf16[512,3072]{1,0:T(8,128)(2,1)S(1)}) fusion(f32[512,3072]{1,0:T(8,128)} %get-tuple-element.156, f32[512,3072]{1,0:T(8,128)} %get-tuple-element.170, f32[3072]{0:T(1024)} %param.31, bf16[512,768]{1,0:T(8,128)(2,1)S(1)} %get-tuple-element.148, bf16[3072,768]{1,0:T(8,128)(2,1)} %param.26), kind=kOutput, calls=%fused_computation.48 | convolution fusion | flops 2442654720 | bytes 21258240 | tf_op jit(solution)/shard_map/dot_general | solution.py:30
  164.4 7.2 multiply_reduce_fusion.2
  178.6 4.2 all-to-all-start.1
  186.7 7.8 %all-to-all-done.1 = bf16[512,4,192]{0,2,1:T(8,128)(2,1)} async-done(((bf16[512,4,192]{0,2,1:T(8,128)(2,1)}), bf16[512,4,192]{0,2,1:T(8,128)(2,1)}, u32[]{:S(2)}, u32[]{:S(2)}) %all-to-all-start.1) | async-done | bytes 786464 | tf_op jit(solution)/shard_map/all_to_all | solution.py:177
  194.5 39.9 %while.24 = (s32[]{:T(128)}, bf16[4,512,3,3,64]{1,4,3,2,0:T(8,128)(2,1)}, bf16[4,512,3,3,64]{1,4,3,2,0:T(8,128)(2,1)}, s32[4]{0:T(128)}, f32[4,3,512,1]{2,1,3,0:...) while((s32[]{:T(128)}, bf16[4,512,3,3,64]{1,4,3,2,0:T(8,128)(2,1)}, ...), condition=%wide.region_16.17_spmd, body=%wide.region_14.16_spmd.sunk | while | flops 512654336 | bytes 27953856 | solution.py:185
  234.5 4.9 copy.63
  239.4 5.9 reshape.345
  245.2 7.0 copy.64
  252.2 53.9 %all_to_all.45 = bf16[2048,3,1,192]{3,1,2,0:T(4,128)(2,1)} all-to-all(bf16[2048,3,1,192]{3,1,2,0:T(4,128)(2,1)} %copy.64), channel_id=1, replica_groups=mesh['batch'=8,'head'=4] {'head'}, dimensions={0} | all-to-all | bytes 4718592 | tf_op jit(solution)/shard_map/all_to_all | solution.py:186
  306.1 7.4 copy.73
  317.1 5.0 convolution_bitcast_fusion
  322.3 8.8 %fusion.48 = f32[768,3072]{0,1:T(8,128)} fusion(bf16[512,3072]{1,0:T(8,128)(2,1)} %copy-done.38, f32[512,768]{1,0:T(8,128)} %copy-done.5, f32[768]{0:T(1024)} %get-tuple-element.107, f32[768]{0:T(1024)S(1)} %copy-done.24, f32[512]{0:T(512)} %copy-done.25, f32[512]{0:T(512)S(1)} %copy-done.15), kind=kOutput, calls=%fused_computation.145 | convolution fusion | flops 2417885184 | bytes 14166016 | tf_op jit(solution)/shard_map/dot_general | solution.py:24
  331.2 8.4 %fusion.61 = f32[3072,768]{0,1:T(8,128)} fusion(bf16[512,3072]{1,0:T(8,128)(2,1)} %copy-done.37, bf16[512,768]{1,0:T(8,128)(2,1)} %copy-done.11), kind=kOutput, calls=%fused_computation.155 | convolution fusion | flops 2415919104 | bytes 13369344 | tf_op jit(solution)/shard_map/dot_general | solution.py:24
  357.9 42.4 %all-reduce.5 = (f32[3,768]{1,0:T(4,128)}, f32[6,768]{1,0:T(8,128)}, f32[2,768]{1,0:T(2,128)}, f32[3072]{0:T(1024)}, f32[768]{0:T(1024)}) all-reduce(f32[3,768]{1,0:T(4,128)S(1)} %broadcast_multiply_fusion.1, f32[6,768]{1,0:T(8,128)} %stack.38, ...), channel_id=7, replica_groups=mesh['batch'=8,'head'=4] {'batch','head'}, use_global_device_ids=true, to_apply=%region_24.25.clone | all-reduce | flops 12288 | bytes 98304
  406.8 5.1 add_convert_fusion.1
  411.9 70.7 %reduce-scatter.9.cloned.1.call-done = f32[768,72]{0,1:T(8,128)} async-done(((f32[768,2304]{0,1:T(8,128)}), f32[768,72]{0,1:T(8,128)}) %reduce-scatter.9.cloned.1.call-update) | async-done | bytes 221200 | tf_op jit(solution)/shard_map/reduce_scatter | solution.py:202
  482.7 142.3 %reduce-scatter.13.cloned.1.call-done = f32[768,96]{0,1:T(8,128)} async-done(((f32[768,3072]{0,1:T(8,128)}), f32[768,96]{0,1:T(8,128)}) %reduce-scatter.13.cloned.1.call-update) | async-done | bytes 294928 | tf_op jit(solution)/shard_map/reduce_scatter | solution.py:204
  625.0 140.9 %reduce-scatter.15.cloned.1.call-done = f32[3072,24]{0,1:T(8,128)} async-done(((f32[3072,768]{0,1:T(8,128)}), f32[3072,24]{0,1:T(8,128)}) %reduce-scatter.15.cloned.1.call-update) | async-done | bytes 294928 | tf_op jit(solution)/shard_map/reduce_scatter | solution.py:205
  (253 shorter events, 162.9 us)
Async XLA Ops:
  8.8 121.2 %copy-start.23 = (f32[768]{0:T(1024)}, f32[768]{0:T(1024)S(1)}, u32[]{:S(2)}) copy-start(f32[768]{0:T(1024)S(1)} %get-tuple-element.180) | copy-start | bytes 9220
  21.4 33.8 %all-to-all-start = ((bf16[512,3,4,192]{0,3,1,2:T(8,128)(2,1)}), bf16[512,3,4,192]{0,3,1,2:T(8,128)(2,1)}, u32[]{:S(2)}, u32[]{:S(2)}) async-start(bf16[512,3,4,192]{0,3,1,2:T(8,128)(2,1)} %copy.60), calls=%async_computation | async-start | bytes 4718592 | tf_op jit(solution)/shard_map/all_to_all | solution.py:115
  26.0 385.9 %reduce-scatter.17.cloned.1.call-start = ((), (), s32[]{:S(2)}) async-start(), calls=%async_computation.12 | async-start | bytes 2433024 | tf_op jit(solution)/shard_map/reduce_scatter | solution.py:206
  90.2 6.4 collective-permute-start
  94.0 7.9 %collective-permute-start.1 = (bf16[512,1,192]{0,2,1:T(8,128)(2,1)}, bf16[512,1,192]{0,2,1:T(8,128)(2,1)S(1)}, u32[]{:S(2)}, u32[]{:S(2)}) collective-permute-start(bf16[512,1,192]{0,2,1:T(8,128)(2,1)} %get-tuple-element.163), channel_id=1, source_target_pairs={{0,2},{1,3},{2,0},{3,1},{4,6},{5,7},{6,4},{7,5},{8,10},{9,11},{10,... | collective-permute-start | bytes 589832 | tf_op jit(solution)/shard_map/ppermute | solution.py:135
  94.8 10.6 %collective-permute-start.2 = (bf16[512,1,192]{0,2,1:T(8,128)(2,1)}, bf16[512,1,192]{0,2,1:T(8,128)(2,1)S(1)}, u32[]{:S(2)}, u32[]{:S(2)}) collective-permute-start(bf16[512,1,192]{0,2,1:T(8,128)(2,1)} %get-tuple-element.162), channel_id=1, source_target_pairs={{0,3},{1,2},{2,1},{3,0},{4,7},{5,6},{6,5},{7,4},{8,11},{9,10},{10,... | collective-permute-start | bytes 589832 | tf_op jit(solution)/shard_map/ppermute | solution.py:135
  106.0 24.0 %slice-start = ((s8[4718592]{0:T(1024)(128)(4,1)}), s8[4194304]{0:T(1024)(128)(4,1)S(1)}, s32[]{:S(2)}) async-start(s8[4718592]{0:T(1024)(128)(4,1)} %bitcast.196), calls=%async_computation.13 | async-start | bytes 8388608
  108.9 21.2 %copy-start.5 = (f32[512,768]{1,0:T(8,128)}, f32[512,768]{1,0:T(8,128)S(1)}, u32[]{:S(2)}) copy-start(f32[512,768]{1,0:T(8,128)S(1)} %get-tuple-element.169) | copy-start | bytes 4718596
  108.9 21.2 %copy-start.14 = (f32[512]{0:T(512)}, f32[512]{0:T(512)S(1)}, u32[]{:S(2)}) copy-start(f32[512]{0:T(512)S(1)} %broadcast_multiply_fusion.3) | copy-start | bytes 6148
  110.0 20.1 %copy-start.25 = (f32[512]{0:T(512)}, f32[512]{0:T(512)S(1)}, u32[]{:S(2)}) copy-start(f32[512]{0:T(512)S(1)} %fusion.43) | copy-start | bytes 6148
  110.0 20.1 %copy-start.30 = (f32[768]{0:T(1024)S(1)}, f32[768]{0:T(1024)}, u32[]{:S(2)}) copy-start(f32[768]{0:T(1024)} %get-tuple-element.106) | copy-start | bytes 9220
  110.0 20.1 %slice-start.1 = ((s8[4718592]{0:T(1024)(128)(4,1)}), s8[524288]{0:T(1024)(128)(4,1)S(1)}, s32[]{:S(2)}) async-start(s8[4718592]{0:T(1024)(128)(4,1)} %bitcast.196), calls=%async_computation.14 | async-start | bytes 1048576
  132.9 10.5 %copy-start.1 = (f32[512,768]{1,0:T(8,128)}, f32[512,768]{1,0:T(8,128)S(1)}, u32[]{:S(2)}) copy-start(f32[512,768]{1,0:T(8,128)S(1)} %get-tuple-element.172) | copy-start | bytes 4718596
  154.8 9.6 %copy-start.11 = (bf16[512,768]{1,0:T(8,128)(2,1)}, bf16[512,768]{1,0:T(8,128)(2,1)S(1)}, u32[]{:S(2)}) copy-start(bf16[512,768]{1,0:T(8,128)(2,1)S(1)} %get-tuple-element.148) | copy-start | bytes 2359300
  154.8 9.6 %copy-start.6 = (f32[512,768]{1,0:T(8,128)S(1)}, f32[512,768]{1,0:T(8,128)}, u32[]{:S(2)}) copy-start(f32[512,768]{1,0:T(8,128)} %copy-done.5) | copy-start | bytes 4718596
  154.8 9.6 %copy-start.8 = (f32[512,768]{1,0:T(8,128)S(1)}, f32[512,768]{1,0:T(8,128)}, u32[]{:S(2)}) copy-start(f32[512,768]{1,0:T(8,128)} %get-tuple-element.154) | copy-start | bytes 4718596
  154.8 9.6 %copy-start.15 = (f32[512]{0:T(512)S(1)}, f32[512]{0:T(512)}, u32[]{:S(2)}) copy-start(f32[512]{0:T(512)} %copy-done.14) | copy-start | bytes 6148
  154.8 9.6 %copy-start.24 = (f32[768]{0:T(1024)S(1)}, f32[768]{0:T(1024)}, u32[]{:S(2)}) copy-start(f32[768]{0:T(1024)} %copy-done.23) | copy-start | bytes 9220
  178.6 15.9 %all-to-all-start.1 = ((bf16[512,4,192]{0,2,1:T(8,128)(2,1)}), bf16[512,4,192]{0,2,1:T(8,128)(2,1)}, u32[]{:S(2)}, u32[]{:S(2)}) async-start(bf16[512,4,192]{0,2,1:T(8,128)(2,1)} %bitcast.195), calls=%async_computation.1 | async-start | bytes 1572864 | tf_op jit(solution)/shard_map/all_to_all | solution.py:177
  182.8 229.1 %reduce-scatter.11.cloned.1.call-start = ((), (), s32[]{:S(2)}) async-start(), calls=%async_computation.9 | async-start | bytes 2433024 | tf_op jit(solution)/shard_map/reduce_scatter | solution.py:203
  186.7 296.0 %reduce-scatter.9.cloned.1.call-start = ((), (), s32[]{:S(2)}) async-start(), calls=%async_computation.8 | async-start | bytes 7299072 | tf_op jit(solution)/shard_map/reduce_scatter | solution.py:202
  322.1 302.9 %reduce-scatter.13.cloned.1.call-start = ((), (), s32[]{:S(2)}) async-start(), calls=%async_computation.10 | async-start | bytes 9732096 | tf_op jit(solution)/shard_map/reduce_scatter | solution.py:204
  331.2 434.7 %reduce-scatter.15.cloned.1.call-start = ((), (), s32[]{:S(2)}) async-start(), calls=%async_computation.11 | async-start | bytes 9732096 | tf_op jit(solution)/shard_map/reduce_scatter | solution.py:205
  340.3 17.7 %copy-start.22 = (f32[768]{0:T(1024)S(1)}, f32[768]{0:T(1024)}, u32[]{:S(2)}) copy-start(f32[768]{0:T(1024)} %get-tuple-element.176) | copy-start | bytes 9220
  (30 other events, 96.4 us)
Sparse Core Ops, SparseCore 0:
  153.3 100.2 reduce-scatter.16
  260.2 98.0 reduce-scatter.10
  364.6 118.0 reduce-scatter.8
  490.0 134.9 reduce-scatter.12
  631.3 134.5 reduce-scatter.14
